TPU v7x, 32 devices: a whole 2x2x4 slice. The times are simulated.
32 devices in a mesh: grp: 2 (over y), pol: 16 (over z, x, core).
Axes of the slice: x: 2, y: 2, z: 4, core: 2. Of those that a mesh axis runs over, the one named last changes fastest.
Arguments:
- shocks: float32 [6, 128, 1024], P('grp'), parts along dimension 0, may hold values from -6 to 6
- loadings: float32 [1024, 128], P('pol'), may hold values from -0.5 to 0.5
- sec_drift: float32 [1024], P('pol'), may hold values from -0.02 to 0.08
- holdings: float32 [1024, 128], P('pol'), may hold values from -0.1875 to 0.1875
- fund_of: int32 [8192, 1], P('pol'), may hold values from 0 to 127
- product_type: int32 [8192], P('pol'), may hold values from 0 to 7
- term_years: int32 [8192], P('pol'), may hold values from 1 to 3
- asset_start: float32 [8192], P('pol'), may hold values from 0.35 to 3
- liab_start: float32 [8192], P('pol'), may hold values from 0.3 to 3
- base_lapse: float32 [8], replicated, may hold values from 0.02 to 0.2
- guarantee: float32 [8], replicated, may hold values from 0 to 0.08
- lapse_draw: bfloat16 [8192, 6, 1024], P('pol', 'grp'), parts along dimension 1, may hold values from 0 to 1
Outputs:
- assets: float32 [8192, 2048], P('pol', 'grp'), parts along dimension 1
- liability: float32 [8192, 2048], P('pol', 'grp'), parts along dimension 1
- credit_rates: float32 [6, 128, 1024], P('grp', None, 'pol'), parts along dimension 0
There are 2 independent parts, one for each index of `grp`. A program takes and returns all parts, laid end to end along the dimension named above; an argument that names none is the same for every part. Nothing has to cross between parts.
Inputs may be any that keep to these rules, and one draw needn't show every extreme that they name: `fund_of`: every fund backs at least one policy.
All inputs are finite; a program needn't handle non-finite values.
Results may differ from a plain program's by a relative error of at most 0.0003.
Values sent between devices are 32-bit elements; how exact they have to be, the bound alone decides.
A program may use at most 64 MiB of HBM per device.

v0:
```python
import jax
import jax.numpy as jnp
from jax import lax
from jax.sharding import PartitionSpec as P


def crediting(totals):
    return 0.01 + jax.nn.softplus(20.0 * (totals[0] / totals[1] - 1.05)) / 20.0


def local(
    shocks,
    loadings,
    sec_drift,
    holdings,
    fund_of,
    product_type,
    term_years,
    asset_start,
    liab_start,
    base_lapse,
    guarantee,
    lapse_draw,
):
    highest = lax.Precision.HIGHEST
    num_years = shocks.shape[0]
    num_paths = shocks.shape[2]
    num_funds = holdings.shape[1]
    sec_ret = (
        0.25 * jnp.tanh(jnp.einsum("sk,ykp->ysp", loadings, shocks, precision=highest))
        + sec_drift[None, :, None]
    )
    partial_funds = jnp.einsum("sf,ysp->yfp", holdings, sec_ret, precision=highest)
    fund_ret = lax.psum(partial_funds, "pol")
    member = (fund_of[:, 0][:, None] == jnp.arange(num_funds, dtype=jnp.int32)[None, :]).astype(
        jnp.float32
    )
    type_hot = (
        product_type[:, None] == jnp.arange(base_lapse.shape[0], dtype=jnp.int32)[None, :]
    ).astype(jnp.float32)
    guaranteed = jnp.sum(type_hot * guarantee[None, :], axis=1)
    base_rate = jnp.sum(type_hot * base_lapse[None, :], axis=1)
    count = asset_start.shape[0]
    assets = jnp.broadcast_to(asset_start[:, None], (count, num_paths))
    liability = jnp.broadcast_to(liab_start[:, None], (count, num_paths))
    owned_paths = num_paths // lax.axis_size("pol")
    first_path = lax.axis_index("pol") * owned_paths
    collected = []
    for year in range(num_years):
        year_ret = fund_ret[year]
        in_force = (term_years > year).astype(jnp.float32)[:, None]
        growth = jnp.dot(member, year_ret, precision=highest)
        assets = assets * (1.0 + in_force * growth)
        fund_sums = jnp.stack(
            [
                jnp.dot(member.T, in_force * assets, precision=highest),
                jnp.dot(member.T, liability, precision=highest),
            ]
        )
        totals = lax.psum(fund_sums, "pol")
        declared = crediting(totals)
        own_rates = lax.dynamic_slice_in_dim(declared, first_path, owned_paths, 1)
        collected.append(own_rates)
        credit = jnp.maximum(jnp.dot(member, declared, precision=highest), guaranteed[:, None])
        lapse_rate = jnp.minimum(
            base_rate[:, None]
            * (0.5 + lapse_draw[:, year, :].astype(jnp.float32))
            * jnp.exp(5.0 * (growth - credit)),
            0.5,
        )
        liability = liability * (1.0 + in_force * credit) * (1.0 - in_force * lapse_rate)
        assets = assets * (1.0 - in_force * lapse_rate)
    return (assets, liability, jnp.stack(collected))


def solution(mesh):
    in_specs = (
        P("grp", None, None),
        P("pol", None),
        P("pol"),
        P("pol", None),
        P("pol", None),
        P("pol"),
        P("pol"),
        P("pol"),
        P("pol"),
        P(),
        P(),
        P("pol", "grp", None),
    )
    out_specs = (P("pol", "grp"), P("pol", "grp"), P("grp", None, "pol"))
    return jax.shard_map(local, mesh=mesh, in_specs=in_specs, out_specs=out_specs, check_vma=False)
```

profile of v0, /device:TPU:0, one launch (start us, length us, event | category | flops | bytes accessed | tf_op | source)
XLA Modules:
  0.0 433.8 jit_solution(17481085283756002193)
XLA Ops:
  7.2 0.0 copy-start
  7.2 0.0 all-reduce.5.cloned.1.call-start
  7.2 1.3 copy-done
  8.6 1.8 fusion.20
  10.4 0.0 copy-start.11
  10.4 3.8 convolution_bitcast_fusion
  14.2 0.0 all-reduce.5.cloned.1.call-update
  14.2 0.0 all-reduce.7.cloned.1.call-start
  14.3 1.6 convolution_bitcast_fusion.3
  15.9 97.1 %all-reduce.5.cloned.1.call-done = f32[3,128,1024]{1,2,0:T(8,128)} async-done(((f32[3,128,1024]{1,2,0:T(8,128)}), f32[3,128,1024]{1,2,0:T(8,128)}) %all-reduce.5.cloned.1.call-update) | async-done | bytes 1572880 | tf_op jit(solution)/shard_map/psum | solution.py:34
  113.0 2.1 fusion.53
  115.1 0.0 copy-start.10
  115.1 1.3 copy-done.7
  116.4 1.3 fusion.27
  117.7 0.0 copy-start.13
  117.7 0.0 copy-start.15
  117.7 1.0 pad_maximum_fusion
  118.8 0.0 all-reduce.7.cloned.1.call-update
  118.8 0.0 all-reduce.9.cloned.1.call-start
  118.9 0.1 select_reduce_fusion.1
  119.0 0.6 copy-done.8
  119.5 2.3 fusion.49
  121.9 89.7 %all-reduce.7.cloned.1.call-done = f32[2,128,1024]{2,1,0:T(8,128)} async-done(((f32[2,128,1024]{2,1,0:T(8,128)}), f32[2,128,1024]{2,1,0:T(8,128)}) %all-reduce.7.cloned.1.call-update) | async-done | bytes 1048592 | tf_op jit(solution)/shard_map/psum | solution.py:60
  211.5 1.6 fusion.37
  213.1 4.7 %multiply_multiply_fusion.2 = (f32[512,1024]{1,0:T(8,128)S(1)}, f32[512,1024]{1,0:T(8,128)S(1)}) fusion(f32[512,1024]{1,0:T(8,128)} %copy-done.7, f32[512]{0:T(512)S(1)} %get-tuple-element.4, f32[512]{0:T(512)S(1)} %get-tuple-element.3, f32[512]{0:T(512)S(1)} %get-tuple-element.11, f32[512]{0:T(512)S(1)} %copy-done.17, bf16[512,3,1024]{2,0,1:T(8,128)(2,1)} %param.23, ...), kind=kOutput, calls=%fused_computation.20 | convolution fusion | flops 816381952 | bytes 9975808 | tf_op jit(solution)/shard_map/dot_general | solution.py:64
  217.9 1.1 fusion.21
  219.0 1.0 convolution_bitcast_fusion.2
  220.0 1.1 pad_maximum_fusion.1
  221.0 0.0 all-reduce.9.cloned.1.call-update
  221.1 0.2 all-reduce.11.cloned.1.call-start
  221.3 2.3 fusion.45
  223.6 90.4 %all-reduce.9.cloned.1.call-done = f32[2,128,1024]{2,1,0:T(8,128)} async-done(((f32[2,128,1024]{2,1,0:T(8,128)}), f32[2,128,1024]{2,1,0:T(8,128)}) %all-reduce.9.cloned.1.call-update) | async-done | bytes 1048592 | tf_op jit(solution)/shard_map/psum | solution.py:60
  314.1 1.6 fusion.39
  315.7 4.2 multiply_multiply_fusion.1
  319.9 1.0 convolution_bitcast_fusion.1
  320.9 2.1 copy-done.2
  323.0 1.3 fusion.24
  324.4 1.1 pad_maximum_fusion.2
  325.5 0.0 all-reduce.11.cloned.1.call-update
  325.5 0.9 constant_dynamic-slice_fusion.2
  326.4 0.1 copy.18
  326.5 92.0 %all-reduce.11.cloned.1.call-done = f32[2,128,1024]{2,1,0:T(8,128)} async-done(((f32[2,128,1024]{2,1,0:T(8,128)}), f32[2,128,1024]{2,1,0:T(8,128)}) %all-reduce.11.cloned.1.call-update) | async-done | bytes 1048592 | tf_op jit(solution)/shard_map/psum | solution.py:60
  418.4 1.6 fusion.41
  420.0 0.1 constant_dynamic-slice_fusion
  420.1 6.3 %multiply_multiply_fusion = (f32[512,1024]{1,0:T(8,128)}, f32[512,1024]{1,0:T(8,128)}) fusion(f32[512,1024]{1,0:T(8,128)} %copy-done.5, f32[512]{0:T(512)S(1)} %get-tuple-element.12, f32[512]{0:T(512)S(1)} %get-tuple-element.4, f32[512,1024]{1,0:T(8,128)} %fusion.45, bf16[512,3,1024]{2,0,1:T(8,128)(2,1)} %param.23, f32[512]{0:T(512)S(1)} %get-tuple-element.3, ...), kind=kOutput, calls=%fused_computation.15 | convolution fusion | flops 815333376 | bytes 14163968 | tf_op jit(solution)/shard_map/dot_general | solution.py:64
  426.5 0.1 copy.19
  426.5 0.1 copy.20
  426.6 0.7 pad_maximum_fusion.3
  (30 shorter events, 0.1 us)
Async XLA Ops:
  7.2 1.4 copy-start
  7.2 3.2 copy-start.12
  7.2 105.8 %all-reduce.5.cloned.1.call-start = ((), (), s32[]{:S(2)}) async-start(), calls=%async_computation | async-start | bytes 3145728 | tf_op jit(solution)/shard_map/psum | solution.py:34
  10.4 3.9 copy-start.11
  10.4 3.9 copy-start.17
  10.4 5.5 %copy-start.14 = (s32[512]{0:T(512)S(1)}, s32[512]{0:T(512)}, u32[]{:S(2)}) copy-start(s32[512]{0:T(512)} %param.18) | copy-start | bytes 6148
  14.2 102.2 %copy-start.18 = (f32[512]{0:T(512)S(1)}, f32[512]{0:T(512)}, u32[]{:S(2)}) copy-start(f32[512]{0:T(512)} %param.19) | copy-start | bytes 6148
  14.2 197.3 %all-reduce.7.cloned.1.call-start = ((), (), s32[]{:S(2)}) async-start(), calls=%async_computation.1 | async-start | bytes 2097152 | tf_op jit(solution)/shard_map/psum | solution.py:60
  115.1 1.3 copy-start.7
  115.1 2.6 copy-start.10
  117.7 1.2 copy-start.13
  117.7 1.2 copy-start.15
  117.7 1.1 copy-start.16
  117.7 1.8 copy-start.8
  118.8 195.3 %all-reduce.9.cloned.1.call-start = ((), (), s32[]{:S(2)}) async-start(), calls=%async_computation.2 | async-start | bytes 2097152 | tf_op jit(solution)/shard_map/psum | solution.py:60
  213.1 4.8 %copy-start.9 = (f32[128,1024]{1,0:T(8,128)}, f32[128,1024]{1,0:T(8,128)S(1)}, u32[]{:S(2)}) copy-start(f32[128,1024]{1,0:T(8,128)S(1)} %fusion.37) | copy-start | bytes 1572868
  217.9 2.1 copy-start.1
  217.9 2.1 copy-start.6
  221.1 197.4 %all-reduce.11.cloned.1.call-start = ((), (), s32[]{:S(2)}) async-start(), calls=%async_computation.3 | async-start | bytes 2097152 | tf_op jit(solution)/shard_map/psum | solution.py:60
  315.7 5.2 %copy-start.3 = (f32[512,1024]{1,0:T(8,128)S(1)}, f32[512,1024]{1,0:T(8,128)}, u32[]{:S(2)}) copy-start(f32[512,1024]{1,0:T(8,128)} %fusion.45) | copy-start | bytes 6291460
  319.9 4.5 %copy-start.4 = (f32[512,1024]{1,0:T(8,128)}, f32[512,1024]{1,0:T(8,128)S(1)}, u32[]{:S(2)}) copy-start(f32[512,1024]{1,0:T(8,128)S(1)} %get-tuple-element.6) | copy-start | bytes 6291460
  319.9 4.5 %copy-start.5 = (f32[512,1024]{1,0:T(8,128)}, f32[512,1024]{1,0:T(8,128)S(1)}, u32[]{:S(2)}) copy-start(f32[512,1024]{1,0:T(8,128)S(1)} %get-tuple-element.5) | copy-start | bytes 6291460
  319.9 3.1 copy-start.2
Sparse Core Ops, SparseCore 0:
  14.4 98.6 all-reduce.4
  118.9 92.5 all-reduce.6
  221.2 92.8 all-reduce.8
  325.6 92.7 all-reduce.10
where the time goes:
time: 434 us
  waiting for transfers between devices  369 us (85%)
  matrix products  34.8 us (8%)
  between operations  14.1 us (3%)
  other arithmetic  8.72 us (2%)
  local copies, waits for them, and re-layouts  6.66 us (2%)
    psum x3, waiting for transfers between devices, local(): totals = lax.psum(fund_sums, 'pol')  272 us
    psum x1, waiting for transfers between devices, local(): fund_ret = lax.psum(partial_funds, 'pol')  97.1 us
    dot_general x3, matrix products, local(): jnp.dot(member, declared, precision=highest)  15.3 us
  transfers between devices with their start and end apart: 4, of which 4 were waited for; matrix products, arithmetic and copies ran while one was open for 2% of the time, Pallas kernels for 0%

commit v1 on v0

--- a/solution.py
+++ b/solution.py
@@ -31,7 +31,10 @@
         + sec_drift[None, :, None]
     )
     partial_funds = jnp.einsum("sf,ysp->yfp", holdings, sec_ret, precision=highest)
-    fund_ret = lax.psum(partial_funds, "pol")
+    routes_all_match = lambda row_data, named_axis: jnp.sum(
+        lax.all_gather(row_data, named_axis), axis=0
+    )
+    fund_ret = routes_all_match(partial_funds, "pol")
     member = (fund_of[:, 0][:, None] == jnp.arange(num_funds, dtype=jnp.int32)[None, :]).astype(
         jnp.float32
     )

time: 434 us -> 477 us (1.099)
  waiting for transfers between devices: 369 us -> 404 us
  other arithmetic: 8.72 us -> 18.1 us
    all_gather x0 -> x1, waiting for transfers between devices: none -> 130 us  [local(): lax.all_gather(row_data, named_axis)]
    psum x1 -> x0, waiting for transfers between devices: 97.1 us -> none  [local(): fund_ret = lax.psum(partial_funds, 'pol')]
    reduce_sum x0 -> x1, other arithmetic: none -> 9.34 us  [local(): jnp.sum(lax.all_gather(row_data, named_axis), axis=0)]
where the time goes in v1:
time: 477 us; the launch traced here: 476 us
  waiting for transfers between devices  404 us (85%)
  matrix products  32.6 us (7%)
  other arithmetic  18.1 us (4%)
  between operations  14.1 us (3%)
  local copies, waits for them, and re-layouts  7.71 us (2%)
    psum x3, waiting for transfers between devices, local(): totals = lax.psum(fund_sums, 'pol')  274 us
    all_gather x1, waiting for transfers between devices, local(): lax.all_gather(row_data, named_axis)  130 us
    dot_general x3, matrix products, local(): jnp.dot(member, declared, precision=highest)  15.3 us
  transfers between devices with their start and end apart: 4, of which 4 were waited for; matrix products, arithmetic and copies ran while one was open for 2% of the time, Pallas kernels for 0%

profile of v1, /device:TPU:0, one launch (start us, length us, event | category | flops | bytes accessed | tf_op | source)
XLA Modules:
  0.0 476.4 jit_solution(7995390864021022172)
XLA Ops:
  7.2 0.0 copy-start
  7.2 0.0 all-gather.3.cloned.1.call-start
  7.2 1.3 copy-done
  8.6 1.8 fusion.20
  10.4 2.6 convolution_bitcast_fusion
  13.1 0.0 copy-start.13
  13.1 1.6 copy.23
  14.7 0.0 all-gather.3.cloned.1.call-update
  14.7 0.0 all-reduce.4.cloned.1.call-start
  14.8 1.6 convolution_bitcast_fusion.3
  16.4 129.7 %all-gather.3.cloned.1.call-done = f32[48,128,1024]{2,1,0:T(8,128)} async-done(((f32[3,128,1024]{2,1,0:T(8,128)}), f32[48,128,1024]{2,1,0:T(8,128)}) %all-gather.3.cloned.1.call-update) | async-done | bytes 25165840 | tf_op jit(solution)/shard_map/all_gather | solution.py:35
  146.1 9.3 %reduce_sum.27 = f32[3,128,1024]{2,1,0:T(8,128)S(1)} reduce(f32[16,3,128,1024]{3,2,1,0:T(8,128)} %bitcast.97, f32[]{:T(128)} %constant.12.clone.1), dimensions={0}, to_apply=%region_0.0 | reduce | flops 5898240 | bytes 26738692 | tf_op jit(solution)/shard_map/reduce_sum | solution.py:34
  155.5 0.0 copy-start.17
  155.5 1.0 fusion.53
  156.5 1.3 copy-done.7
  157.8 1.3 fusion.27
  159.1 0.0 copy-start.12
  159.2 1.1 pad_maximum_fusion
  160.2 0.0 all-reduce.4.cloned.1.call-update
  160.2 0.2 all-reduce.6.cloned.1.call-start
  160.5 0.1 select_reduce_fusion.1
  160.6 2.4 fusion.49
  162.9 91.2 %all-reduce.4.cloned.1.call-done = f32[2,128,1024]{2,1,0:T(8,128)} async-done(((f32[2,128,1024]{2,1,0:T(8,128)}), f32[2,128,1024]{2,1,0:T(8,128)}) %all-reduce.4.cloned.1.call-update) | async-done | bytes 1048592 | tf_op jit(solution)/shard_map/psum | solution.py:63
  254.1 1.6 fusion.37
  255.7 4.7 multiply_multiply_fusion.2
  260.5 1.1 fusion.21
  261.6 1.0 convolution_bitcast_fusion.2
  262.6 1.1 pad_maximum_fusion.1
  263.6 0.0 all-reduce.6.cloned.1.call-update
  263.7 0.0 all-reduce.8.cloned.1.call-start
  263.7 2.4 fusion.45
  266.1 90.6 %all-reduce.6.cloned.1.call-done = f32[2,128,1024]{2,1,0:T(8,128)} async-done(((f32[2,128,1024]{2,1,0:T(8,128)}), f32[2,128,1024]{2,1,0:T(8,128)}) %all-reduce.6.cloned.1.call-update) | async-done | bytes 1048592 | tf_op jit(solution)/shard_map/psum | solution.py:63
  356.7 1.6 fusion.39
  358.3 4.2 multiply_multiply_fusion.1
  362.5 1.0 convolution_bitcast_fusion.1
  363.5 2.1 copy-done.2
  365.6 1.3 fusion.24
  367.0 1.1 pad_maximum_fusion.2
  368.1 0.0 all-reduce.8.cloned.1.call-update
  368.1 0.9 constant_dynamic-slice_fusion.2
  369.0 0.1 copy.25
  369.1 91.9 %all-reduce.8.cloned.1.call-done = f32[2,128,1024]{2,1,0:T(8,128)} async-done(((f32[2,128,1024]{2,1,0:T(8,128)}), f32[2,128,1024]{2,1,0:T(8,128)}) %all-reduce.8.cloned.1.call-update) | async-done | bytes 1048592 | tf_op jit(solution)/shard_map/psum | solution.py:63
  461.0 1.6 fusion.41
  462.6 0.1 constant_dynamic-slice_fusion
  462.7 6.3 %multiply_multiply_fusion = (f32[512,1024]{1,0:T(8,128)}, f32[512,1024]{1,0:T(8,128)}) fusion(f32[512,1024]{1,0:T(8,128)} %copy-done.5, f32[512]{0:T(512)S(1)} %get-tuple-element.12, f32[512]{0:T(512)S(1)} %get-tuple-element.4, f32[512,1024]{1,0:T(8,128)} %fusion.45, bf16[512,3,1024]{2,0,1:T(8,128)(2,1)} %param.23, f32[512]{0:T(512)S(1)} %get-tuple-element.3, ...), kind=kOutput, calls=%fused_computation.15 | convolution fusion | flops 815333376 | bytes 14163968 | tf_op jit(solution)/shard_map/dot_general | solution.py:67
  469.1 0.1 copy.26
  469.2 0.1 copy.27
  469.2 0.7 pad_maximum_fusion.3
  (30 shorter events, 0.1 us)
Async XLA Ops:
  7.2 1.4 copy-start
  7.2 3.2 copy-start.11
  7.2 138.9 %all-gather.3.cloned.1.call-start = ((), (), s32[]{:S(2)}) async-start(), calls=%async_computation.3 | async-start | bytes 26738688 | tf_op jit(solution)/shard_map/all_gather | solution.py:35
  13.0 1.7 copy-start.10
  13.0 1.7 copy-start.16
  13.1 3.3 copy-start.13
  14.7 239.4 %all-reduce.4.cloned.1.call-start = ((), (), s32[]{:S(2)}) async-start(), calls=%async_computation | async-start | bytes 2097152 | tf_op jit(solution)/shard_map/psum | solution.py:63
  155.5 2.4 copy-start.17
  156.5 1.3 copy-start.7
  156.5 2.6 copy-start.9
  159.1 1.4 copy-start.12
  159.1 1.4 copy-start.14
  159.1 1.4 copy-start.15
  160.2 196.5 %all-reduce.6.cloned.1.call-start = ((), (), s32[]{:S(2)}) async-start(), calls=%async_computation.1 | async-start | bytes 2097152 | tf_op jit(solution)/shard_map/psum | solution.py:63
  255.7 4.8 copy-start.8
  260.5 2.1 copy-start.1
  260.5 2.1 copy-start.6
  263.7 197.4 %all-reduce.8.cloned.1.call-start = ((), (), s32[]{:S(2)}) async-start(), calls=%async_computation.2 | async-start | bytes 2097152 | tf_op jit(solution)/shard_map/psum | solution.py:63
  358.3 5.2 %copy-start.3 = (f32[512,1024]{1,0:T(8,128)S(1)}, f32[512,1024]{1,0:T(8,128)}, u32[]{:S(2)}) copy-start(f32[512,1024]{1,0:T(8,128)} %fusion.45) | copy-start | bytes 6291460
  362.5 4.5 copy-start.4
  362.5 4.5 copy-start.5
  362.5 3.1 copy-start.2
Sparse Core Ops, SparseCore 0:
  14.8 131.2 all-gather.2
  160.4 93.7 all-reduce.3
  263.8 92.8 all-reduce.5
  368.2 92.7 all-reduce.7
